TPU v7x, 512 devices: a whole 4x4x16 slice. The times are simulated.
512 devices in a mesh: rows: 64 (over x, z), cols: 8 (over y, core).
Axes of the slice: x: 4, y: 4, z: 16, core: 2. Of those that a mesh axis runs over, the one named last changes fastest.
Arguments:
- sketch: bfloat16 [131072, 256], P(('rows', 'cols')), may hold values from -6 to 6
- blocks: bfloat16 [4096, 256, 256], P(('rows', 'cols')), may hold values from -0.375 to 0.375
- block_rows: int32 [4096], P(('rows', 'cols')), may hold values from 0 to 3, as said below
- block_cols: int32 [4096], P(('rows', 'cols')), may hold values from 0 to 63
- counts: int32 [512], P(('rows', 'cols')), may hold values from 1 to 8, as said below
Outputs:
- basis: float32 [65536, 256], P(('rows', 'cols'))
- factor: float32 [256, 256], replicated
Inputs may be any that keep to these rules, and one draw needn't show every extreme that they name: Within one device's 8 slots the pairs (block_rows, block_cols) are distinct. `counts`: some device has exactly 8 live slots.
All inputs are finite; a program needn't handle non-finite values.
Results may differ from a plain program's by a relative error of at most 0.0003.
Values may be sent and summed in bfloat16 or wider, within the bound.
A program may use at most 64 MiB of HBM per device.

v0:
```python
import jax
import jax.numpy as jnp
from jax import lax
from jax.sharding import PartitionSpec as P

RB = 4


def local(sketch, blocks, block_rows, block_cols, counts):
    highest = lax.Precision.HIGHEST
    slots, width, _ = blocks.shape
    columns = sketch.shape[1]
    live_count = counts[0]
    starts = block_cols * width
    panel = lax.all_gather(sketch, "rows", axis=0, tiled=True)
    chosen = jax.vmap(lambda offset: lax.dynamic_slice_in_dim(panel, offset, width, 0))(starts)
    products = jnp.einsum("bij,bjk->bik", blocks, chosen, preferred_element_type=jnp.float32)
    selector = (
        (block_rows[:, None] == jnp.arange(RB, dtype=jnp.int32)[None, :])
        & (jnp.arange(slots, dtype=jnp.int32) < live_count)[:, None]
    ).astype(jnp.float32)
    partial_rows = jnp.einsum("br,bik->rik", selector, products, precision=highest)
    partial_rows = partial_rows.reshape(RB * width, columns)
    total_rows = RB * width * lax.axis_size("rows")
    slab_total = lax.psum(partial_rows, "cols")
    gram_matrix = lax.psum(jnp.dot(slab_total.T, slab_total, precision=highest), "rows")
    share_rows = slab_total.shape[0] // lax.axis_size("cols")
    own_rows = lax.dynamic_slice_in_dim(
        slab_total, lax.axis_index("cols") * share_rows, share_rows, 0
    )
    lower_factor = jnp.linalg.cholesky(gram_matrix)
    root_rows = jnp.sqrt(jnp.float32(total_rows))
    solved = lax.linalg.triangular_solve(
        lower_factor, own_rows, left_side=False, lower=True, transpose_a=True
    )
    return (solved * root_rows, lower_factor.T / root_rows)


def solution(mesh):
    in_specs = (
        P(("rows", "cols"), None),
        P(("rows", "cols"), None, None),
        P(("rows", "cols")),
        P(("rows", "cols")),
        P(("rows", "cols")),
    )
    out_specs = (P(("rows", "cols"), None), P())
    return jax.shard_map(local, mesh=mesh, in_specs=in_specs, out_specs=out_specs, check_vma=False)
```

profile of v0, /device:TPU:8, one launch (start us, length us, event | category | flops | bytes accessed | tf_op | source)
XLA Modules:
  0.0 611.1 jit_solution(694707326038857665)
XLA Ops:
  9.3 162.0 %all-gather.2.cloned.1.call-done = bf16[16384,256]{1,0:T(8,128)(2,1)} async-done(((bf16[256,256]{1,0:T(8,128)(2,1)}), bf16[16384,256]{1,0:T(8,128)(2,1)}) %all-gather.2.cloned.1.call-update) | async-done | bytes 8388624 | tf_op jit(solution)/shard_map/all_gather | solution.py:15
  171.3 17.0 %while.2 = (s32[]{:T(128)}, bf16[16384,256]{1,0:T(8,128)(2,1)}, s32[8,2]{0,1:T(2,128)S(1)}, bf16[8,256,256]{2,1,0:T(8,128)(2,1)S(1)}, s32[]{:T(128)}) while((s32[]{:T(128)}, bf16[16384,256]{1,0:T(8,128)(2,1)}, s32[8,2]{0,1:T(2,128)S(1)}, bf16[8,256,256]{2,1,0:T(8,128)(2,1)S(1)}, s32[]{:T(128)}) %tuple.41), condition=%wide.while_cond, body=%wide.while_body.sunk | while | flops 2 | bytes 262241 | solution.py:16
  171.9 1.5 bitcast_dynamic-update-slice_fusion.4
  174.0 1.5 bitcast_dynamic-update-slice_fusion.4
  176.2 1.5 bitcast_dynamic-update-slice_fusion.4
  178.3 1.5 bitcast_dynamic-update-slice_fusion.4
  180.4 1.5 bitcast_dynamic-update-slice_fusion.4
  182.6 1.5 bitcast_dynamic-update-slice_fusion.4
  184.7 1.5 bitcast_dynamic-update-slice_fusion.4
  186.8 1.5 bitcast_dynamic-update-slice_fusion.4
  188.4 1.8 fusion.19
  190.2 2.2 copy.16
  193.5 1.2 copy.11
  195.0 70.9 %all-reduce.5.cloned.1.call-done = f32[1024,256]{1,0:T(8,128)} async-done(((f32[1024,256]{1,0:T(8,128)}), f32[1024,256]{1,0:T(8,128)}) %all-reduce.5.cloned.1.call-update) | async-done | bytes 1048592 | tf_op jit(solution)/shard_map/psum | solution.py:25
  265.9 4.1 fusion.20
  270.0 268.6 %all-reduce.7.cloned.1.call-done = f32[256,256]{0,1:T(8,128)} async-done(((f32[256,256]{0,1:T(8,128)}), f32[256,256]{0,1:T(8,128)}) %all-reduce.7.cloned.1.call-update) | async-done | bytes 262160 | tf_op jit(solution)/shard_map/psum | solution.py:26
  540.6 11.7 %cholesky.50 = f32[128,128]{1,0:T(8,128)S(1)} custom-call(f32[128,128]{1,0:T(8,128)S(1)} %cholesky.118), custom_call_target="Cholesky" | custom-call | tf_op jit(solution)/shard_map/jit(cholesky)/cholesky | solution.py:31
  552.4 9.8 %custom-call.14 = f32[1,128,128]{1,2,0:T(8,128)S(1)} custom-call(f32[1,128,128]{2,1,0:T(8,128)S(1)} %get-tuple-element.45), custom_call_target="InvertDiagBlocksLowerTriangular" | custom-call | tf_op jit(solution)/shard_map/jit(cholesky)/cholesky | solution.py:31
  562.7 11.7 %cholesky.105 = f32[128,128]{1,0:T(8,128)S(1)} custom-call(f32[128,128]{1,0:T(8,128)S(1)} %convolution_subtract_fusion.1), custom_call_target="Cholesky" | custom-call | tf_op jit(solution)/shard_map/jit(cholesky)/cholesky | solution.py:31
  576.7 4.0 while.3
  577.3 1.4 bitcast_dynamic-update-slice_fusion.5
  579.3 1.4 bitcast_dynamic-update-slice_fusion.5
  580.7 19.7 %custom-call.15 = f32[2,128,128]{1,2,0:T(8,128)S(1)} custom-call(f32[2,128,128]{2,1,0:T(8,128)S(1)} %get-tuple-element.17), custom_call_target="InvertDiagBlocksLowerTriangular" | custom-call | tf_op jit(solution)/shard_map/triangular_solve | solution.py:33
  601.5 1.1 convolution_subtract_fusion
  (53 shorter events, 15.3 us)
Async XLA Ops:
  7.2 181.2 %copy-start = (bf16[8,256,256]{2,1,0:T(8,128)(2,1)S(1)}, bf16[8,256,256]{2,1,0:T(8,128)(2,1)}, u32[]{:S(2)}) copy-start(bf16[8,256,256]{2,1,0:T(8,128)(2,1)} %param.6) | copy-start | bytes 3145732
  7.2 164.1 %all-gather.2.cloned.1.call-start = ((), (), s32[]{:S(2)}) async-start(), calls=%async_computation | async-start | bytes 8519680 | tf_op jit(solution)/shard_map/all_gather | solution.py:15
  7.9 258.0 %all-reduce.5.cloned.1.call-start = ((), (), s32[]{:S(2)}) async-start(), calls=%async_computation.1 | async-start | bytes 2097152 | tf_op jit(solution)/shard_map/psum | solution.py:25
  190.2 2.2 copy-start.1
  194.8 343.8 %all-reduce.7.cloned.1.call-start = ((), (), s32[]{:S(2)}) async-start(), calls=%async_computation.2 | async-start | bytes 524288 | tf_op jit(solution)/shard_map/psum | solution.py:26
Sparse Core Ops, SparseCore 0:
  10.9 160.3 all-gather.1
  194.9 70.9 all-reduce.4
  270.1 268.4 all-reduce.6
where the time goes:
time: 612 us; the launch traced here: 611 us
  waiting for transfers between devices  502 us (82%)
  other arithmetic  55.5 us (9%)
  local copies, waits for them, and re-layouts  27 us (4%)
  between operations  15.9 us (3%)
  matrix products  10 us (2%)
    psum x1, waiting for transfers between devices, local(): lax.psum(jnp.dot(slab_total.T, slab_total, precision=highest), 'rows')  269 us
    all_gather x1, waiting for transfers between devices, local(): panel = lax.all_gather(sketch, 'rows', axis=0, tiled=True)  162 us
    psum x1, waiting for transfers between devices, local(): slab_total = lax.psum(partial_rows, 'cols')  70.9 us
    another operation x6, other arithmetic, local(): lower_factor = jnp.linalg.cholesky(gram_matrix)  34.2 us
    another operation x2, other arithmetic, local(): lax.linalg.triangular_solve(lower_factor, own_rows, left_side=False, lowe...  19.7 us
    gather x24, local copies, waits for them, and re-layouts  16.9 us
  transfers between devices with their start and end apart: 3, of which 3 were waited for; matrix products, arithmetic and copies ran while one was open for 0% of the time, Pallas kernels for 0%

commit v1 on v0

--- a/solution.py
+++ b/solution.py
@@ -22,7 +22,11 @@
     partial_rows = jnp.einsum("br,bik->rik", selector, products, precision=highest)
     partial_rows = partial_rows.reshape(RB * width, columns)
     total_rows = RB * width * lax.axis_size("rows")
-    slab_total = lax.psum(partial_rows, "cols")
+    slab_total = partial_rows
+    for hop in (1, 2, 4):
+        slab_total = slab_total + lax.ppermute(
+            slab_total, "cols", [(dev, dev ^ hop) for dev in range(8)]
+        )
     gram_matrix = lax.psum(jnp.dot(slab_total.T, slab_total, precision=highest), "rows")
     share_rows = slab_total.shape[0] // lax.axis_size("cols")
     own_rows = lax.dynamic_slice_in_dim(

time: 612 us -> 591 us (0.966)
  waiting for transfers between devices: 502 us -> 475 us
  starting transfers between devices: 0.3 us -> 8.83 us
    psum x1 -> x0, waiting for transfers between devices: 70.9 us -> none  [local(): slab_total = lax.psum(partial_rows, 'cols')]
    ppermute x0 -> x3, waiting for transfers between devices: none -> 50.6 us  [local(): lax.ppermute(slab_total, 'cols', [(dev, dev ^ hop) for dev in range(8)])]
    ppermute x0 -> x3, starting transfers between devices: none -> 8.76 us  [local(): lax.ppermute(slab_total, 'cols', [(dev, dev ^ hop) for dev in range(8)])]
    psum x1, waiting for transfers between devices: 269 us -> 262 us  [local(): lax.psum(jnp.dot(slab_total.T, slab_total, precision=highest), 'rows')]
  transfers between devices with their start and end apart: 3 -> 5, of which waited for: 3 -> 5; matrix products, arithmetic and copies ran while one was open for 0% -> 0% of each run, Pallas kernels for 0% -> 0%
where the time goes in v1:
time: 591 us; the launch traced here: 590 us
  waiting for transfers between devices  475 us (80%)
  other arithmetic  55.9 us (9%)
  local copies, waits for them, and re-layouts  27.3 us (5%)
  between operations  16.2 us (3%)
  starting transfers between devices  8.83 us (1%)
  matrix products  6.76 us (1%)
    psum x1, waiting for transfers between devices, local(): lax.psum(jnp.dot(slab_total.T, slab_total, precision=highest), 'rows')  262 us
    all_gather x1, waiting for transfers between devices, local(): panel = lax.all_gather(sketch, 'rows', axis=0, tiled=True)  162 us
    ppermute x3, waiting for transfers between devices, local(): lax.ppermute(slab_total, 'cols', [(dev, dev ^ hop) for dev in range(8)])  50.6 us
    another operation x6, other arithmetic, local(): lower_factor = jnp.linalg.cholesky(gram_matrix)  34.1 us
    another operation x2, other arithmetic, local(): lax.linalg.triangular_solve(lower_factor, own_rows, left_side=False, lowe...  19.7 us
    gather x24, local copies, waits for them, and re-layouts  18.2 us
  transfers between devices with their start and end apart: 5, of which 5 were waited for; matrix products, arithmetic and copies ran while one was open for 0% of the time, Pallas kernels for 0%

profile of v1, /device:TPU:8, one launch (start us, length us, event | category | flops | bytes accessed | tf_op | source)
XLA Modules:
  0.0 590.0 jit_solution(13805066172462341186)
XLA Ops:
  9.3 162.0 %all-gather.2.cloned.1.call-done = bf16[16384,256]{1,0:T(8,128)(2,1)} async-done(((bf16[256,256]{1,0:T(8,128)(2,1)}), bf16[16384,256]{1,0:T(8,128)(2,1)}) %all-gather.2.cloned.1.call-update) | async-done | bytes 8388624 | tf_op jit(solution)/shard_map/all_gather | solution.py:15
  171.3 18.3 %while.2 = (s32[]{:T(128)}, bf16[16384,256]{1,0:T(8,128)(2,1)}, s32[8,2]{0,1:T(2,128)S(1)}, bf16[8,256,256]{2,1,0:T(8,128)(2,1)S(1)}, s32[]{:T(128)}) while((s32[]{:T(128)}, bf16[16384,256]{1,0:T(8,128)(2,1)}, s32[8,2]{0,1:T(2,128)S(1)}, bf16[8,256,256]{2,1,0:T(8,128)(2,1)S(1)}, s32[]{:T(128)}) %tuple.41), condition=%wide.while_cond, body=%wide.while_body.sunk | while | flops 2 | bytes 262241 | solution.py:16
  172.0 1.6 bitcast_dynamic-update-slice_fusion.4
  174.3 1.6 bitcast_dynamic-update-slice_fusion.4
  176.6 1.6 bitcast_dynamic-update-slice_fusion.4
  178.8 1.6 bitcast_dynamic-update-slice_fusion.4
  181.1 1.6 bitcast_dynamic-update-slice_fusion.4
  185.7 1.6 bitcast_dynamic-update-slice_fusion.4
  188.0 1.6 bitcast_dynamic-update-slice_fusion.4
  189.7 1.8 fusion.20
  191.5 2.2 copy.16
  195.0 1.9 collective-permute-start
  197.0 2.6 collective-permute-done
  199.7 2.5 collective-permute-start.1
  202.2 24.6 %collective-permute-done.1 = f32[1024,256]{1,0:T(8,128)S(1)} collective-permute-done((f32[1024,256]{1,0:T(8,128)S(1)}, f32[1024,256]{1,0:T(8,128)S(1)}, u32[]{:S(2)}, u32[]{:S(2)}) %collective-permute-start.1) | collective-permute-done | bytes 1048608 | tf_op jit(solution)/shard_map/ppermute | solution.py:27
  227.0 4.3 collective-permute-start.2
  231.3 23.4 %collective-permute-done.2 = f32[1024,256]{1,0:T(8,128)S(1)} collective-permute-done((f32[1024,256]{1,0:T(8,128)S(1)}, f32[1024,256]{1,0:T(8,128)S(1)}, u32[]{:S(2)}, u32[]{:S(2)}) %collective-permute-start.2) | collective-permute-done | bytes 1048608 | tf_op jit(solution)/shard_map/ppermute | solution.py:27
  254.8 2.5 fusion.21
  257.4 261.5 %all-reduce.4.cloned.1.call-done = f32[256,256]{0,1:T(8,128)} async-done(((f32[256,256]{0,1:T(8,128)}), f32[256,256]{0,1:T(8,128)}) %all-reduce.4.cloned.1.call-update) | async-done | bytes 262160 | tf_op jit(solution)/shard_map/psum | solution.py:30
  521.0 11.7 %cholesky.50 = f32[128,128]{1,0:T(8,128)S(1)} custom-call(f32[128,128]{1,0:T(8,128)S(1)} %cholesky.118), custom_call_target="Cholesky" | custom-call | tf_op jit(solution)/shard_map/jit(cholesky)/cholesky | solution.py:35
  532.8 9.8 %custom-call.14 = f32[1,128,128]{1,2,0:T(8,128)S(1)} custom-call(f32[1,128,128]{2,1,0:T(8,128)S(1)} %get-tuple-element.45), custom_call_target="InvertDiagBlocksLowerTriangular" | custom-call | tf_op jit(solution)/shard_map/jit(cholesky)/cholesky | solution.py:35
  543.1 11.8 %cholesky.105 = f32[128,128]{1,0:T(8,128)S(1)} custom-call(f32[128,128]{1,0:T(8,128)S(1)} %convolution_subtract_fusion), custom_call_target="Cholesky" | custom-call | tf_op jit(solution)/shard_map/jit(cholesky)/cholesky | solution.py:35
  557.0 3.9 while.3
  561.0 19.7 %custom-call.15 = f32[2,128,128]{1,2,0:T(8,128)S(1)} custom-call(f32[2,128,128]{2,1,0:T(8,128)S(1)} %get-tuple-element.17), custom_call_target="InvertDiagBlocksLowerTriangular" | custom-call | tf_op jit(solution)/shard_map/triangular_solve | solution.py:37
  (59 shorter events, 19.8 us)
Async XLA Ops:
  7.2 182.5 %copy-start = (bf16[8,256,256]{2,1,0:T(8,128)(2,1)S(1)}, bf16[8,256,256]{2,1,0:T(8,128)(2,1)}, u32[]{:S(2)}) copy-start(bf16[8,256,256]{2,1,0:T(8,128)(2,1)} %param.6) | copy-start | bytes 3145732
  7.2 164.1 %all-gather.2.cloned.1.call-start = ((), (), s32[]{:S(2)}) async-start(), calls=%async_computation | async-start | bytes 8519680 | tf_op jit(solution)/shard_map/all_gather | solution.py:15
  7.9 511.0 %all-reduce.4.cloned.1.call-start = ((), (), s32[]{:S(2)}) async-start(), calls=%async_computation.1 | async-start | bytes 524288 | tf_op jit(solution)/shard_map/psum | solution.py:30
  191.5 2.2 copy-start.1
  195.0 4.6 collective-permute-start
  199.7 27.1 %collective-permute-start.1 = (f32[1024,256]{1,0:T(8,128)S(1)}, f32[1024,256]{1,0:T(8,128)S(1)}, u32[]{:S(2)}, u32[]{:S(2)}) collective-permute-start(f32[1024,256]{1,0:T(8,128)S(1)} %bitcast_add_fusion.1), channel_id=1, source_target_pairs={{0,2},{1,3},{2,0},{3,1},{4,6},{5,7},{6,4},{7,5},{8,10},{9,11},{10,... | collective-permute-start | bytes 3145736 | tf_op jit(solution)/shard_map/ppermute | solution.py:27
  227.0 27.7 %collective-permute-start.2 = (f32[1024,256]{1,0:T(8,128)S(1)}, f32[1024,256]{1,0:T(8,128)S(1)}, u32[]{:S(2)}, u32[]{:S(2)}) collective-permute-start(f32[1024,256]{1,0:T(8,128)S(1)} %add.43), channel_id=1, source_target_pairs={{0,4},{1,5},{2,6},{3,7},{4,0},{5,1},{6,2},{7,3},{8,12},{9,13},{10,... | collective-permute-start | bytes 3145736 | tf_op jit(solution)/shard_map/ppermute | solution.py:27
Sparse Core Ops, SparseCore 0:
  10.9 160.3 all-gather.1
  257.5 261.3 all-reduce.3
